TPU v7x, 32 devices: a whole 2x2x4 slice. The times are simulated.
32 devices in a mesh: prow: 2 (over core), pcol: 16 (over z, y, x).
Axes of the slice: x: 2, y: 2, z: 4, core: 2. Of those that a mesh axis runs over, the one named last changes fastest.
Arguments:
- factor_rows: float32 [8, 256, 24, 2048], P(None, 'prow', None, 'pcol'), as said below
- sensitivity: float32 [1024, 24, 2048], P('prow', None, 'pcol'), may hold values from -6 to 6
- pivots: int32 [2048], replicated, may hold values from 0 to 2047, as said below
Outputs:
- adjoint: float32 [1024, 8, 256], P(None, None, 'prow')
- updated: float32 [1024, 24, 2048], P('prow', None, 'pcol')
Inputs may be any that keep to these rules, and one draw needn't show every extreme that they name: pivots is a permutation of the first 2048 columns. `factor_rows`: in M, the entries left of each block row's diagonal block are zero and each diagonal block is lower triangular.
All inputs are finite; a program needn't handle non-finite values.
Results may differ from a plain program's by a relative error of at most 0.0001.
Values sent between devices are 32-bit elements; how exact they have to be, the bound alone decides.
No kernel may reach another device: no remote copies, remote signals or barrier semaphores. Data moves between devices by JAX's collectives and lax.ppermute only.
A program may use at most 192 MiB of HBM per device.

v0:
```python
import jax
import jax.numpy as jnp
from jax import lax
from jax.sharding import PartitionSpec as P

NB = 1024


def shards(factor_rows, sensitivity, pivots):
    pcol_count = lax.axis_size("pcol")
    row_cycles = factor_rows.shape[0]
    half_cycles = row_cycles // 2
    tile_width = factor_rows.shape[1]
    col_tiles = factor_rows.shape[2]
    local_rhs = sensitivity.shape[0]
    per_block = NB // tile_width
    pcol_index = lax.axis_index("pcol")
    tile_ids = jnp.arange(col_tiles) * pcol_count + pcol_index
    stripe_cols = pcol_count * tile_width
    gathered = lax.all_gather(sensitivity[:, :1, :], "pcol", axis=2, tiled=True)
    flat_cols = gathered.reshape(local_rhs, stripe_cols)
    swapped = jnp.take(flat_cols, pivots, axis=1)
    merged = swapped.reshape(local_rhs, 1, pcol_count, tile_width)
    own_tiles = lax.dynamic_index_in_dim(merged, pcol_index, 2, keepdims=False)
    working = jnp.concatenate([own_tiles, sensitivity[:, 1:, :]], axis=1)

    def tile_range(section):
        return (
            section * per_block // pcol_count,
            ((section + 1) * per_block - 1) // pcol_count + 1,
        )

    def solve_block(working, section):
        low_tile, high_tile = tile_range(section)
        chosen = tile_ids[low_tile:high_tile]
        inside = ((chosen >= section * per_block) & (chosen < (section + 1) * per_block)).astype(
            jnp.float32
        )
        masked = working[:, low_tile:high_tile, :] * inside[None, :, None]
        all_rhs = lax.all_gather(masked, "prow", axis=0, tiled=True)
        inverse_tiles = factor_rows[
            section * half_cycles : (section + 1) * half_cycles, :, low_tile:high_tile, :
        ]
        partial_sum = jnp.einsum(
            "hbu,atbu->hat",
            all_rhs,
            inverse_tiles,
            precision=lax.Precision.HIGHEST,
            preferred_element_type=jnp.float32,
        )
        partial_sum = partial_sum.reshape(all_rhs.shape[0], half_cycles * tile_width)
        return lax.psum(partial_sum, "pcol")

    solved_first = solve_block(working, 0)
    low_tile, high_tile = tile_range(1)
    next_tiles = high_tile - low_tile
    first_rows = factor_rows[:half_cycles, :, low_tile:high_tile, :].reshape(
        half_cycles * tile_width, next_tiles * tile_width
    )
    picked = solved_first
    early = lax.psum_scatter(
        jnp.dot(
            picked, first_rows, precision=lax.Precision.HIGHEST, preferred_element_type=jnp.float32
        ),
        "prow",
        scatter_dimension=0,
        tiled=True,
    ).reshape(local_rhs, next_tiles, tile_width)
    chosen = tile_ids[low_tile:high_tile]
    inside = ((chosen >= per_block) & (chosen < 2 * per_block)).astype(jnp.float32)
    working = working.at[:, low_tile:high_tile, :].add(-early * inside[None, :, None])
    solved_second = solve_block(working, 1)
    both_solved = jnp.concatenate([solved_first, solved_second], axis=1)
    all_rows = factor_rows.reshape(row_cycles * tile_width, col_tiles * tile_width)
    picked = both_solved
    change = lax.psum_scatter(
        jnp.dot(
            picked, all_rows, precision=lax.Precision.HIGHEST, preferred_element_type=jnp.float32
        ),
        "prow",
        scatter_dimension=0,
        tiled=True,
    ).reshape(local_rhs, col_tiles, tile_width)
    keep_cols = (tile_ids >= 2 * per_block).astype(jnp.float32)
    working = working - change * keep_cols[None, :, None]
    adjoint = jnp.concatenate([solved_first, solved_second], axis=1).reshape(
        solved_first.shape[0], row_cycles, tile_width
    )
    return (adjoint, working)


def solution(mesh):
    return jax.shard_map(
        shards,
        mesh=mesh,
        in_specs=(P(None, "prow", None, "pcol"), P("prow", None, "pcol"), P()),
        out_specs=(P(None, None, "prow"), P("prow", None, "pcol")),
        check_vma=False,
    )
```

profile of v0, /device:TPU:0, one launch (start us, length us, event | category | flops | bytes accessed | tf_op | source)
XLA Modules:
  0.0 478.7 jit_solution(9994754397476234976)
XLA Ops:
  7.2 1.7 slice.41
  8.9 0.8 copy.11
  9.8 0.0 all-reduce.3.cloned.1.call-start
  9.9 0.7 and_bitcast_fusion
  10.7 0.7 fusion.4
  11.4 2.5 fusion.5
  13.9 76.2 %all-gather.3.cloned.1.call-done = f32[512,1,2048]{0,2,1:T(8,128)} async-done(((f32[512,1,128]{0,2,1:T(8,128)}), f32[512,1,2048]{0,2,1:T(8,128)}) %all-gather.3.cloned.1.call-update) | async-done | bytes 4194320 | tf_op jit(solution)/shard_map/all_gather | solution.py:20
  90.2 11.7 %gather_fusion = f32[2048,512]{1,0:T(8,128)} fusion(f32[512,2048]{0,1:T(8,128)} %bitcast.40, s32[2048]{0:T(1024)S(1)} %fusion.4), kind=kCustom, calls=%fused_computation | custom fusion | bytes 8396800 | tf_op jit(solution)/shard_map/jit(_take)/gather | solution.py:22
  101.8 1.0 constant_dynamic-slice_fusion.1
  102.8 0.1 copy.12
  103.0 2.2 all_gather.10
  105.2 3.1 fusion.6
  108.3 0.0 reduce-scatter.3.cloned.1.call-start
  108.4 124.7 %all-reduce.3.cloned.1.call-done = f32[1024,512]{1,0:T(8,128)} async-done(((f32[1024,512]{1,0:T(8,128)}), f32[1024,512]{1,0:T(8,128)}) %all-reduce.3.cloned.1.call-update) | async-done | bytes 2097168 | tf_op jit(solution)/shard_map/psum | solution.py:52
  233.0 4.2 fusion.7
  237.2 0.0 all-reduce.5.cloned.1.call-start
  237.4 7.3 %reduce-scatter.3.cloned.1.call-done = f32[512,128]{1,0:T(8,128)} async-done(((f32[1024,128]{1,0:T(8,128)}), f32[512,128]{1,0:T(8,128)}) %reduce-scatter.3.cloned.1.call-update) | async-done | bytes 262160 | tf_op jit(solution)/shard_map/reduce_scatter | solution.py:61
  244.7 1.0 broadcast_multiply_fusion
  245.7 2.2 all-gather
  247.9 3.1 fusion.8
  251.0 0.2 reduce-scatter.5.cloned.1.call-start
  251.2 1.6 constant_dynamic-update-slice_fusion.1
  252.8 125.4 %all-reduce.5.cloned.1.call-done = f32[1024,512]{1,0:T(8,128)} async-done(((f32[1024,512]{1,0:T(8,128)}), f32[1024,512]{1,0:T(8,128)}) %all-reduce.5.cloned.1.call-update) | async-done | bytes 2097168 | tf_op jit(solution)/shard_map/psum | solution.py:52
  378.3 3.2 constant_dynamic-update-slice_fusion
  381.4 60.8 %fusion = f32[1024,3072]{1,0:T(8,128)} fusion(f32[1024,1024]{1,0:T(8,128)} %constant_dynamic-update-slice_fusion, f32[128,8,24,128]{3,2,1,0:T(8,128)} %bitcast.55), kind=kOutput, calls=%fused_computation.1 | convolution fusion | flops 38654705664 | bytes 29360128 | tf_op jit(solution)/shard_map/dot_general | solution.py:77
  442.2 3.4 slice.45
  445.6 4.0 pad_maximum_fusion
  449.6 8.2 %scatter-add.4 = f32[512,24,128]{2,1,0:T(8,128)} dynamic-update-slice(f32[512,24,128]{2,1,0:T(8,128)} %pad_maximum_fusion, f32[512,1,128]{2,1,0:T(1,128)S(1)} %bitcast.52, s32[]{:T(128)} %constant.48.clone.1, s32[]{:T(128)} %constant.48.clone.1, s32[]{:T(128)} %constant.48.clone.1) | dynamic-update-slice | bytes 524292 | tf_op jit(solution)/shard_map/scatter-add | solution.py:71
  457.8 6.1 %copy.13 = f32[128,8,8,128]{3,2,1,0:T(8,128)} copy(f32[128,8,8,128]{3,1,2,0:T(8,128)} %bitcast.43) | data formatting | bytes 8388608
  464.0 4.3 copy.15
  468.3 0.3 slice-done.1
  468.6 3.6 fusion.3
  (18 shorter events, 0.2 us)
Async XLA Ops:
  7.2 83.0 %all-gather.3.cloned.1.call-start = ((), (), s32[]{:S(2)}) async-start(), calls=%async_computation.2 | async-start | bytes 4456448 | tf_op jit(solution)/shard_map/all_gather | solution.py:20
  9.8 223.2 %all-reduce.3.cloned.1.call-start = ((), (), s32[]{:S(2)}) async-start(), calls=%async_computation.3 | async-start | bytes 4194304 | tf_op jit(solution)/shard_map/psum | solution.py:52
  108.3 136.4 %reduce-scatter.3.cloned.1.call-start = ((), (), s32[]{:S(2)}) async-start(), calls=%async_computation.4 | async-start | bytes 786432 | tf_op jit(solution)/shard_map/reduce_scatter | solution.py:61
  237.2 14.0 %copy-start = (f32[1024,512]{1,0:T(8,128)S(1)}, f32[1024,512]{1,0:T(8,128)}, u32[]{:S(2)}) copy-start(f32[1024,512]{1,0:T(8,128)} %all-reduce.3.cloned.1.call-done) | copy-start | bytes 6291460
  237.2 141.0 %all-reduce.5.cloned.1.call-start = ((), (), s32[]{:S(2)}) async-start(), calls=%async_computation.5 | async-start | bytes 4194304 | tf_op jit(solution)/shard_map/psum | solution.py:52
  251.0 213.0 %reduce-scatter.5.cloned.1.call-start = ((), (), s32[]{:S(2)}) async-start(), calls=%async_computation.6 | async-start | bytes 18874368 | tf_op jit(solution)/shard_map/reduce_scatter | solution.py:76
  464.0 4.4 slice-start
  464.0 4.7 slice-start.1
Sparse Core Ops, SparseCore 0:
  11.3 78.7 all-gather.2
  108.4 124.5 all-reduce.2
  237.4 7.2 reduce-scatter.2
  251.1 127.1 all-reduce.4
  442.4 20.8 reduce-scatter.4
where the time goes:
time: 479 us
  waiting for transfers between devices  334 us (70%)
  matrix products  71.2 us (15%)
  local copies, waits for them, and re-layouts  45.1 us (9%)
  between operations  14 us (3%)
  other arithmetic  9.97 us (2%)
    psum x2, waiting for transfers between devices, solve_block(): return lax.psum(partial_sum, 'pcol')  250 us
    all_gather x1, waiting for transfers between devices, shards(): gathered = lax.all_gather(sensitivity[:, :1, :], 'pcol', axis=2, tiled=True)  76.2 us
    dot_general x1, matrix products, shards(): jnp.dot(picked, all_rows, precision=lax.Precision.HIGHEST, preferred_elem...  60.8 us
    unnamed x11, local copies, waits for them, and re-layouts  13.4 us
    gather x1, local copies, waits for them, and re-layouts, shards(): swapped = jnp.take(flat_cols, pivots, axis=1)  11.7 us
  transfers between devices with their start and end apart: 5, of which 4 were waited for; matrix products, arithmetic and copies ran while one was open for 6% of the time, Pallas kernels for 0%

commit v1 on v0

--- a/solution.py
+++ b/solution.py
@@ -49,7 +49,7 @@
             preferred_element_type=jnp.float32,
         )
         partial_sum = partial_sum.reshape(all_rhs.shape[0], half_cycles * tile_width)
-        return lax.psum(partial_sum, "pcol")
+        return jnp.sum(lax.all_gather(partial_sum, axis_name="pcol"), axis=0)
 
     solved_first = solve_block(working, 0)
     low_tile, high_tile = tile_range(1)

time: 479 us -> 951 us (1.99)
  waiting for transfers between devices: 334 us -> 784 us
  other arithmetic: 9.97 us -> 38.9 us
    all_gather x0 -> x2, waiting for transfers between devices: none -> 702 us  [solve_block(): return jnp.sum(lax.all_gather(partial_sum, axis_name='pcol'), axis=0)]
    psum x2 -> x0, waiting for transfers between devices: 250 us -> none  [solve_block(): return lax.psum(partial_sum, 'pcol')]
    reduce_sum x0 -> x2, other arithmetic: none -> 26.8 us  [solve_block(): return jnp.sum(lax.all_gather(partial_sum, axis_name='pcol'), axis=0)]
  transfers between devices with their start and end apart: 5 -> 5, of which waited for: 4 -> 4; matrix products, arithmetic and copies ran while one was open for 6% -> 3% of each run, Pallas kernels for 0% -> 0%
where the time goes in v1:
time: 951 us; the launch traced here: 950 us
  waiting for transfers between devices  784 us (82%)
  matrix products  71.4 us (8%)
  other arithmetic  38.9 us (4%)
  local copies, waits for them, and re-layouts  37.2 us (4%)
  between operations  14 us (1%)
    all_gather x2, waiting for transfers between devices, solve_block(): return jnp.sum(lax.all_gather(partial_sum, axis_name='pcol'), axis=0)  702 us
    all_gather x1, waiting for transfers between devices, shards(): gathered = lax.all_gather(sensitivity[:, :1, :], 'pcol', axis=2, tiled=True)  76.2 us
    dot_general x1, matrix products, shards(): jnp.dot(picked, all_rows, precision=lax.Precision.HIGHEST, preferred_elem...  62.6 us
    reduce_sum x2, other arithmetic, solve_block(): return jnp.sum(lax.all_gather(partial_sum, axis_name='pcol'), axis=0)  26.8 us
  transfers between devices with their start and end apart: 5, of which 4 were waited for; matrix products, arithmetic and copies ran while one was open for 3% of the time, Pallas kernels for 0%

profile of v1, /device:TPU:0, one launch (start us, length us, event | category | flops | bytes accessed | tf_op | source)
XLA Modules:
  0.0 950.2 jit_solution(9593303263309133836)
XLA Ops:
  7.2 1.7 slice.41
  8.9 0.8 copy.11
  9.8 0.0 all-gather.9.cloned.1.call-start
  9.9 0.7 and_bitcast_fusion
  10.7 0.7 fusion.5
  11.4 2.5 fusion.7
  13.9 76.2 %all-gather.7.cloned.1.call-done = f32[512,1,2048]{0,2,1:T(8,128)} async-done(((f32[512,1,128]{0,2,1:T(8,128)}), f32[512,1,2048]{0,2,1:T(8,128)}) %all-gather.7.cloned.1.call-update) | async-done | bytes 4194320 | tf_op jit(solution)/shard_map/all_gather | solution.py:20
  90.2 11.7 %gather_fusion = f32[2048,512]{1,0:T(8,128)} fusion(f32[512,2048]{0,1:T(8,128)} %bitcast.42, s32[2048]{0:T(1024)S(1)} %fusion.5), kind=kCustom, calls=%fused_computation | custom fusion | bytes 8396800 | tf_op jit(solution)/shard_map/jit(_take)/gather | solution.py:22
  101.8 1.0 constant_dynamic-slice_fusion.1
  102.8 0.1 copy.12
  103.0 2.2 all_gather.16
  105.2 3.1 fusion.8
  108.3 0.0 reduce-scatter.3.cloned.1.call-start
  108.4 349.6 %all-gather.9.cloned.1.call-done = f32[16384,512]{1,0:T(8,128)} async-done(((f32[1024,512]{1,0:T(8,128)}), f32[16384,512]{1,0:T(8,128)}) %all-gather.9.cloned.1.call-update) | async-done | bytes 33554448 | tf_op jit(solution)/shard_map/all_gather | solution.py:52
  457.9 12.7 %reduce_sum.18 = f32[1024,512]{1,0:T(8,128)S(1)} reduce(f32[16,1024,512]{2,1,0:T(8,128)} %bitcast.44, f32[]{:T(128)} %constant.57.clone.1), dimensions={0}, to_apply=%region_0.1 | reduce | flops 7864320 | bytes 35651588 | tf_op jit(solution)/shard_map/reduce_sum | solution.py:52
  470.7 2.6 fusion.9
  473.4 6.2 reduce-scatter.3.cloned.1.call-done
  479.6 1.0 broadcast_multiply_fusion
  480.6 2.2 all-gather.1
  482.8 3.1 fusion.10
  485.9 0.2 reduce-scatter.5.cloned.1.call-start
  486.1 351.9 %all-gather.11.cloned.1.call-done = f32[16384,512]{1,0:T(8,128)} async-done(((f32[1024,512]{1,0:T(8,128)}), f32[16384,512]{1,0:T(8,128)}) %all-gather.11.cloned.1.call-update) | async-done | bytes 33554448 | tf_op jit(solution)/shard_map/all_gather | solution.py:52
  838.1 14.0 %reduce_sum.19 = f32[1024,512]{1,0:T(8,128)} reduce(f32[16,1024,512]{2,1,0:T(8,128)} %bitcast.43, f32[]{:T(128)} %constant.57.clone.1), dimensions={0}, to_apply=%region_2.3 | reduce | flops 7864320 | bytes 35651588 | tf_op jit(solution)/shard_map/reduce_sum | solution.py:52
  852.1 62.6 %fusion = f32[1024,3072]{1,0:T(8,128)} fusion(f32[128,8,24,128]{3,2,1,0:T(8,128)} %bitcast.58, f32[1024,512]{1,0:T(8,128)} %reduce_sum.19, f32[1024,512]{1,0:T(8,128)S(1)} %reduce_sum.18), kind=kOutput, calls=%fused_computation.1 | convolution fusion | flops 38655754240 | bytes 29360128 | tf_op jit(solution)/shard_map/dot_general | solution.py:77
  914.7 3.4 slice.45
  918.1 3.5 pad_maximum_fusion
  921.6 8.3 scatter-add.4
  929.8 2.6 fusion.4
  932.5 3.0 copy.13
  935.5 4.3 copy.15
  939.8 0.3 slice-done.1
  940.2 3.6 fusion.3
  (17 shorter events, 0.2 us)
Async XLA Ops:
  7.2 83.0 %all-gather.7.cloned.1.call-start = ((), (), s32[]{:S(2)}) async-start(), calls=%async_computation.2 | async-start | bytes 4456448 | tf_op jit(solution)/shard_map/all_gather | solution.py:20
  9.8 448.1 %all-gather.9.cloned.1.call-start = ((), (), s32[]{:S(2)}) async-start(), calls=%async_computation.5 | async-start | bytes 35651584 | tf_op jit(solution)/shard_map/all_gather | solution.py:52
  108.3 371.3 %reduce-scatter.3.cloned.1.call-start = ((), (), s32[]{:S(2)}) async-start(), calls=%async_computation.3 | async-start | bytes 786432 | tf_op jit(solution)/shard_map/reduce_scatter | solution.py:61
  473.3 364.8 %all-gather.11.cloned.1.call-start = ((), (), s32[]{:S(2)}) async-start(), calls=%async_computation.6 | async-start | bytes 35651584 | tf_op jit(solution)/shard_map/all_gather | solution.py:52
  485.9 449.6 %reduce-scatter.5.cloned.1.call-start = ((), (), s32[]{:S(2)}) async-start(), calls=%async_computation.4 | async-start | bytes 18874368 | tf_op jit(solution)/shard_map/reduce_scatter | solution.py:76
  935.5 4.4 slice-start
  935.5 4.7 slice-start.1
Sparse Core Ops, SparseCore 0:
  11.3 78.7 all-gather.6
  108.4 349.4 all-gather.8
  473.4 6.1 reduce-scatter.2
  486.0 352.0 all-gather.10
  914.8 19.6 reduce-scatter.4
